TPU v7x, 256 devices: a whole 4x4x8 slice. The times are simulated.
256 devices in a mesh: ctx: 32 (over z, y), head: 8 (over x, core).
Axes of the slice: x: 4, y: 4, z: 8, core: 2. Of those that a mesh axis runs over, the one named last changes fastest.
Arguments:
- queries: bfloat16 [2048, 2048], P(None, 'head'), may hold values from -16 to 16
- prefix_keys: bfloat16 [32768, 2048], P('ctx', 'head'), may hold values from -6 to 6
- prefix_values: bfloat16 [32768, 2048], P('ctx', 'head'), may hold values from -6 to 6
- out_grad: bfloat16 [2048, 2048], P(None, 'head'), may hold values from -6 to 6
- block_lists: int32 [16, 16, 64], P('head'), may hold values from 0 to 511, as said below
- list_counts: int32 [16, 16], P('head'), may hold values from 32 to 64
Outputs:
- query_grad: bfloat16 [2048, 2048], P('ctx', 'head')
- key_grad: bfloat16 [32768, 2048], P(('ctx', 'head'))
- value_grad: bfloat16 [32768, 2048], P(('ctx', 'head'))
Inputs may be any that keep to these rules, and one draw needn't show every extreme that they name: `block_lists`: within a list all 64 entries are distinct block numbers; entries from list_counts on are ignored. Of the live entries of every list at most 8 lie in the blocks of one context slice (slice c holds blocks c * 16 onward), and exactly 8 in one slice.
All inputs are finite; a program needn't handle non-finite values.
Results may differ from a plain program's by a relative error of at most 0.017.
Values may be sent and summed in bfloat16 or wider, within the bound.
A program may use at most 128 MiB of HBM per device.

v0:
```python
import jax
import jax.numpy as jnp
from jax import lax
from jax.sharding import PartitionSpec as P

HD = 128
TILE = 128
BLOCK = 64
masked_score = -1e30


def joined(value, axis, join):
    pieces = jax.tree.map(lambda part: lax.all_gather(part, axis), value)
    head = jax.tree.map(lambda part: part[0], pieces)
    tail = jax.tree.map(lambda part: part[1:], pieces)
    running, _ = lax.scan(lambda running, piece: (join(running, piece), None), head, tail)
    return running


def pair_combine(former, latter):
    joint = jnp.maximum(former[0], latter[0])
    return (joint, former[1] * jnp.exp(former[0] - joint) + latter[1] * jnp.exp(latter[0] - joint))


def local(queries, prefix_keys, prefix_values, out_grad, block_lists, list_counts):
    heads_here = prefix_keys.shape[1] // HD
    slice_len = prefix_keys.shape[0]
    blocks_here = slice_len // BLOCK
    latents = queries.shape[0]
    score_scale = HD ** (-0.5)
    local_ids = block_lists - lax.axis_index("ctx") * blocks_here
    positions = jnp.arange(block_lists.shape[2], dtype=jnp.int32)
    listed = (
        (positions[None, None, :] < list_counts[:, :, None])
        & (local_ids >= 0)
        & (local_ids < blocks_here)
    )
    block_ids = jnp.arange(blocks_here, dtype=jnp.int32)
    chosen = jnp.any(listed[..., None] & (local_ids[..., None] == block_ids), axis=2)
    kept = []
    maxima = []
    totals = []
    for head_index in range(heads_here):
        first_col = head_index * HD
        query_head = queries[:, first_col : first_col + HD]
        key_head = prefix_keys[:, first_col : first_col + HD]
        value_head = prefix_values[:, first_col : first_col + HD]
        grad_head = out_grad[:, first_col : first_col + HD]
        key_mask = jnp.repeat(jnp.repeat(chosen[head_index], TILE, axis=0), BLOCK, axis=1)
        key_use = key_head
        value_use = value_head
        query_use = query_head
        grad_use = grad_head
        scores = score_scale * jnp.einsum(
            "ld,sd->ls", query_head, key_head, preferred_element_type=jnp.float32
        )
        dprobs = jnp.einsum("ld,sd->ls", grad_head, value_head, preferred_element_type=jnp.float32)
        scores = jnp.where(key_mask, scores, masked_score)
        row_max = jnp.max(scores, axis=-1)
        weights = jnp.where(key_mask, jnp.exp(scores - row_max[..., None]), 0.0)
        maxima.append(row_max)
        totals.append(jnp.sum(weights, axis=-1))
        kept.append((scores, dprobs, key_mask, key_use, value_use, query_use, grad_use))
    row_maxima = jnp.stack(maxima)
    row_totals = jnp.stack(totals)
    prob_list = []
    merged_max, merged_total = joined((row_maxima, row_totals), "ctx", pair_combine)
    log_totals = merged_max + jnp.log(merged_total)
    partial_deltas = []
    for head_index in range(heads_here):
        scores, dprobs, key_mask = (kept[head_index][0], kept[head_index][1], kept[head_index][2])
        log_here = log_totals[head_index][..., None]
        attn_probs = jnp.where(key_mask, jnp.exp(scores - log_here), 0.0)
        prob_list.append(attn_probs)
        partial_deltas.append(jnp.sum(attn_probs * dprobs, axis=-1))
    row_deltas = lax.psum(jnp.stack(partial_deltas), "ctx")
    query_terms = []
    key_terms = []
    value_terms = []
    for head_index in range(heads_here):
        scores, dprobs, key_mask, key_use, value_use, query_use, grad_use = kept[head_index]
        attn_probs = prob_list[head_index]
        delta_here = row_deltas[head_index][..., None]
        dscores = (attn_probs * (dprobs - delta_here)).astype(jnp.bfloat16)
        probs_low = attn_probs.astype(jnp.bfloat16)
        query_terms.append(
            score_scale
            * jnp.einsum("ls,sd->ld", dscores, key_use, preferred_element_type=jnp.float32)
        )
        key_terms.append(
            score_scale
            * jnp.einsum("ls,ld->sd", dscores, query_use, preferred_element_type=jnp.float32)
        )
        value_terms.append(
            jnp.einsum("ls,ld->sd", probs_low, grad_use, preferred_element_type=jnp.float32)
        )
    query_term = jnp.concatenate(query_terms, axis=1)
    key_local = jnp.concatenate(key_terms, axis=1).astype(jnp.bfloat16)
    value_local = jnp.concatenate(value_terms, axis=1).astype(jnp.bfloat16)
    own_rows = latents // lax.axis_size("ctx")
    summed = lax.psum(query_term, "ctx")
    query_grad = lax.dynamic_slice_in_dim(summed, lax.axis_index("ctx") * own_rows, own_rows, 0)
    key_grad, value_grad = (
        lax.all_to_all(key_local, "head", split_axis=0, concat_axis=1, tiled=True),
        lax.all_to_all(value_local, "head", split_axis=0, concat_axis=1, tiled=True),
    )
    return (query_grad.astype(jnp.bfloat16), key_grad, value_grad)


def solution(mesh):
    return jax.shard_map(
        local,
        mesh=mesh,
        in_specs=(
            P(None, "head"),
            P("ctx", "head"),
            P("ctx", "head"),
            P(None, "head"),
            P("head", None, None),
            P("head", None),
        ),
        out_specs=(P("ctx", "head"), P(("ctx", "head"), None), P(("ctx", "head"), None)),
        check_vma=False,
    )
```

profile of v0, /device:TPU:2, one launch (start us, length us, event | category | flops | bytes accessed | tf_op | source)
XLA Modules:
  0.0 488.2 jit_solution(2884194299780184191)
XLA Ops:
  0.7 0.9 fusion.39
  2.7 2.4 fusion.5
  5.1 1.3 fusion.4
  6.5 52.8 %all-gather.2 = f32[32,2,2048]{2,1,0:T(2,128)S(1)} all-gather(f32[1,2,2048]{2,1,0:T(2,128)S(1)} %maximum_bitcast_fusion), channel_id=2, replica_groups=mesh['ctx'=32,'head'=8] {'ctx'}, dimensions={0}, use_global_device_ids=true | all-gather | bytes 540672 | tf_op jit(solution)/shard_map/all_gather | solution.py:13
  59.4 2.1 fusion.3
  61.4 2.1 fusion.2
  63.5 48.3 %all-gather.3 = f32[32,2,2048]{2,1,0:T(2,128)S(1)} all-gather(f32[1,2,2048]{2,1,0:T(2,128)S(1)} %maximum_bitcast_fusion.1), channel_id=3, replica_groups=mesh['ctx'=32,'head'=8] {'ctx'}, dimensions={0}, use_global_device_ids=true | all-gather | bytes 540672 | tf_op jit(solution)/shard_map/all_gather | solution.py:13
  111.9 1.9 while.12
  113.9 9.2 %multiply_reduce_fusion = (f32[2048]{0:T(1024)S(1)}, f32[2048,1024]{0,1:T(8,128)}, f32[2048,1024]{0,1:T(8,128)}) fusion(f32[2048]{0:T(1024)S(1)} %bitcast.110, f32[2048,1024]{0,1:T(8,128)} %copy-done.1, pred[2048,16]{0,1:T(8,128)(4,1)S(1)} %bitcast.98, bf16[1024,256]{1,0:T(8,128)(2,1)} %param.10, bf16[2048,256]{1,0:T(8,128)(2,1)S(1)} %copy-done.3), kind=kOutput, calls=%fused_computation.15 | convolution fusion | flops 549451776 | bytes 26001408 | tf_op jit(solution)/shard_map/ld,sd->ls/dot_general | solution.py:57
  123.1 9.2 %multiply_reduce_fusion.1 = (f32[2048]{0:T(1024)S(1)}, f32[2048,1024]{0,1:T(8,128)}, f32[2048,1024]{0,1:T(8,128)}) fusion(f32[2048]{0:T(1024)S(1)} %bitcast.107, f32[2048,1024]{0,1:T(8,128)} %copy-done, pred[2048,16]{0,1:T(8,128)(4,1)S(1)} %bitcast.95, bf16[1024,256]{1,0:T(8,128)(2,1)S(1)} %copy-done.6, bf16[2048,256]{1,0:T(8,128)(2,1)S(1)} %copy-done.3), kind=kOutput, calls=%fused_computation.16 | convolution fusion | flops 549451776 | bytes 26001408 | tf_op jit(solution)/shard_map/ld,sd->ls/dot_general | solution.py:57
  132.2 140.5 %psum.14 = f32[2,2048]{1,0:T(2,128)S(1)} all-reduce(f32[2,2048]{1,0:T(2,128)S(1)} %pad_maximum_fusion.3), channel_id=1, replica_groups=mesh['ctx'=32,'head'=8] {'ctx'}, use_global_device_ids=true, to_apply=%region_9.10 | all-reduce | flops 4096 | bytes 32768 | tf_op jit(solution)/shard_map/psum | solution.py:76
  272.8 8.0 %multiply_convert_fusion = bf16[2048,1024]{0,1:T(8,128)(2,1)S(1)} fusion(f32[2048,1024]{0,1:T(8,128)} %get-tuple-element.57, f32[2048,1024]{0,1:T(8,128)} %get-tuple-element.70, f32[2048]{0:T(1024)S(1)} %bitcast.112), kind=kLoop, calls=%fused_computation.13 | loop fusion | flops 6291456 | bytes 20979712 | tf_op jit(solution)/shard_map/convert_element_type | solution.py:84
  280.8 2.7 fusion.17
  283.4 10.0 %multiply_convert_fusion.1 = bf16[2048,1024]{0,1:T(8,128)(2,1)} fusion(f32[2048,1024]{0,1:T(8,128)} %get-tuple-element.55, f32[2048,1024]{0,1:T(8,128)} %get-tuple-element.71, f32[2048]{0:T(1024)S(1)} %bitcast.109), kind=kLoop, calls=%fused_computation.14 | loop fusion | flops 6291456 | bytes 20979712 | tf_op jit(solution)/shard_map/convert_element_type | solution.py:84
  293.4 3.5 fusion.16
  297.8 4.8 all-to-all-start
  302.6 3.0 convolution_multiply_fusion
  305.6 3.1 convolution_multiply_fusion.1
  308.7 4.8 fusion.13
  313.7 1.2 fusion.10
  315.8 4.8 all-to-all-start.1
  320.7 163.2 %all-reduce.1 = bf16[2048,256]{0,1:T(8,128)(2,1)} all-reduce(f32[2048,256]{0,1:T(8,128)S(1)} %pad_maximum_fusion), channel_id=1, replica_groups=mesh['ctx'=32,'head'=8] {'ctx'}, use_global_device_ids=true, to_apply=%region_10.11 | all-reduce | flops 524288 | bytes 3145728 | tf_op jit(solution)/shard_map/psum | solution.py:101
  483.8 0.9 dynamic-slice_convert_fusion
  485.5 1.9 copy.20
  (75 shorter events, 6.3 us)
Async XLA Ops:
  0.6 4.5 copy-start.4
  0.6 4.5 copy-start.5
  5.1 56.3 %copy-start.1 = (f32[2048,1024]{0,1:T(8,128)}, f32[2048,1024]{0,1:T(8,128)S(1)}, u32[]{:S(2)}) copy-start(f32[2048,1024]{0,1:T(8,128)S(1)} %get-tuple-element.67) | copy-start | bytes 25165828
  6.5 57.0 %copy-start = (f32[2048,1024]{0,1:T(8,128)}, f32[2048,1024]{0,1:T(8,128)S(1)}, u32[]{:S(2)}) copy-start(f32[2048,1024]{0,1:T(8,128)S(1)} %get-tuple-element.69) | copy-start | bytes 25165828
  59.3 54.5 %copy-start.3 = (bf16[2048,256]{1,0:T(8,128)(2,1)S(1)}, bf16[2048,256]{1,0:T(8,128)(2,1)}, u32[]{:S(2)}) copy-start(bf16[2048,256]{1,0:T(8,128)(2,1)} %param.11) | copy-start | bytes 3145732
  113.8 9.2 %copy-start.6 = (bf16[1024,256]{1,0:T(8,128)(2,1)S(1)}, bf16[1024,256]{1,0:T(8,128)(2,1)}, u32[]{:S(2)}) copy-start(bf16[1024,256]{1,0:T(8,128)(2,1)} %param.10) | copy-start | bytes 1572868
  280.8 12.6 %copy-start.2 = (bf16[2048,1024]{0,1:T(8,128)(2,1)}, bf16[2048,1024]{0,1:T(8,128)(2,1)S(1)}, u32[]{:S(2)}) copy-start(bf16[2048,1024]{0,1:T(8,128)(2,1)S(1)} %multiply_convert_fusion) | copy-start | bytes 12582916
  297.8 18.0 %all-to-all-start = ((bf16[8,128,256]{2,1,0:T(8,128)(2,1)}), bf16[8,128,256]{2,1,0:T(8,128)(2,1)}, u32[]{:S(2)}, u32[]{:S(2)}) async-start(bf16[8,128,256]{2,1,0:T(8,128)(2,1)} %pad_maximum_fusion.1), calls=%async_computation | async-start | bytes 1048576 | tf_op jit(solution)/shard_map/all_to_all | solution.py:104
  305.6 8.1 %slice-start = ((s8[8388608]{0:T(1024)(128)(4,1)}), s8[4194304]{0:T(1024)(128)(4,1)S(1)}, s32[]{:S(2)}) async-start(s8[8388608]{0:T(1024)(128)(4,1)} %bitcast.88), calls=%async_computation.2 | async-start | bytes 8388608
  308.7 5.0 %slice-start.1 = ((s8[8388608]{0:T(1024)(128)(4,1)}), s8[4194304]{0:T(1024)(128)(4,1)S(1)}, s32[]{:S(2)}) async-start(s8[8388608]{0:T(1024)(128)(4,1)} %bitcast.88), calls=%async_computation.3 | async-start | bytes 8388608
  315.8 171.5 %all-to-all-start.1 = ((bf16[8,128,256]{2,1,0:T(8,128)(2,1)}), bf16[8,128,256]{2,1,0:T(8,128)(2,1)S(1)}, u32[]{:S(2)}, u32[]{:S(2)}) async-start(bf16[8,128,256]{2,1,0:T(8,128)(2,1)} %pad_maximum_fusion.2), calls=%async_computation.1 | async-start | bytes 1048576 | tf_op jit(solution)/shard_map/all_to_all | solution.py:105
where the time goes:
time: 489 us; the launch traced here: 488 us
  blocking collectives  405 us (83%)
  matrix products  40.4 us (8%)
  other arithmetic  27.1 us (6%)
  starting transfers between devices  9.64 us (2%)
  local copies, waits for them, and re-layouts  4.93 us (1%)
    psum x1, blocking collectives, local(): summed = lax.psum(query_term, 'ctx')  163 us
    psum x1, blocking collectives, local(): row_deltas = lax.psum(jnp.stack(partial_deltas), 'ctx')  141 us
    all_gather x2, blocking collectives, joined(): pieces = jax.tree.map(lambda part: lax.all_gather(part, axis), value)  101 us
    dot_general x2, matrix products, local(): jnp.einsum('ld,sd->ls', grad_head, value_head, preferred_element_type=jnp...  18.4 us
    convert_element_type x2, other arithmetic, local(): dscores = (attn_probs * (dprobs - delta_here)).astype(jnp.bfloat16)  17.9 us
  transfers between devices with their start and end apart: 2, of which 0 were waited for; matrix products, arithmetic and copies ran while one was open for 3% of the time, Pallas kernels for 0%

commit v1 on v0

--- a/solution.py
+++ b/solution.py
@@ -98,7 +98,12 @@
     key_local = jnp.concatenate(key_terms, axis=1).astype(jnp.bfloat16)
     value_local = jnp.concatenate(value_terms, axis=1).astype(jnp.bfloat16)
     own_rows = latents // lax.axis_size("ctx")
-    summed = lax.psum(query_term, "ctx")
+    world_n = lax.axis_size("ctx")
+    summed = query_term
+    for i0 in [k0 for k0 in (1, 2, 4, 8, 16) if k0 < world_n]:
+        z_new = tuple(((c, c ^ i0) for c in range(world_n)))
+        local_next = lax.ppermute(summed, "ctx", z_new)
+        summed = summed + local_next
     query_grad = lax.dynamic_slice_in_dim(summed, lax.axis_index("ctx") * own_rows, own_rows, 0)
     key_grad, value_grad = (
         lax.all_to_all(key_local, "head", split_axis=0, concat_axis=1, tiled=True),

time: 489 us -> 540 us (1.10)
  waiting for transfers between devices: 0.01 us -> 211 us
  blocking collectives: 405 us -> 242 us
    ppermute x0 -> x5, waiting for transfers between devices: none -> 203 us  [local(): local_next = lax.ppermute(summed, 'ctx', z_new)]
    psum x1 -> x0, blocking collectives: 163 us -> none  [local(): summed = lax.psum(query_term, 'ctx')]
    all_to_all x1, waiting for transfers between devices: 0.01 us -> 8.05 us  [local(): lax.all_to_all(value_local, 'head', split_axis=0, concat_axis=1, tiled=True)]
  transfers between devices with their start and end apart: 2 -> 7, of which waited for: 0 -> 6; matrix products, arithmetic and copies ran while one was open for 3% -> 3% of each run, Pallas kernels for 0% -> 0%
where the time goes in v1:
time: 540 us
  blocking collectives  242 us (45%)
  waiting for transfers between devices  211 us (39%)
  matrix products  38.5 us (7%)
  other arithmetic  30.8 us (6%)
  starting transfers between devices  13.4 us (2%)
    ppermute x5, waiting for transfers between devices, local(): local_next = lax.ppermute(summed, 'ctx', z_new)  203 us
    psum x1, blocking collectives, local(): row_deltas = lax.psum(jnp.stack(partial_deltas), 'ctx')  141 us
    all_gather x2, blocking collectives, joined(): pieces = jax.tree.map(lambda part: lax.all_gather(part, axis), value)  101 us
    dot_general x2, matrix products, local(): jnp.einsum('ld,sd->ls', grad_head, value_head, preferred_element_type=jnp...  18.3 us
    convert_element_type x2, other arithmetic, local(): dscores = (attn_probs * (dprobs - delta_here)).astype(jnp.bfloat16)  17.9 us
  transfers between devices with their start and end apart: 7, of which 6 were waited for; matrix products, arithmetic and copies ran while one was open for 3% of the time, Pallas kernels for 0%

profile of v1, /device:TPU:2, one launch (start us, length us, event | category | flops | bytes accessed | tf_op | source)
XLA Modules:
  0.0 539.9 jit_solution(12304093968775266587)
XLA Ops:
  2.7 2.4 fusion.5
  6.5 52.8 %all-gather.2 = f32[32,2,2048]{2,1,0:T(2,128)S(1)} all-gather(f32[1,2,2048]{2,1,0:T(2,128)S(1)} %maximum_bitcast_fusion), channel_id=2, replica_groups=mesh['ctx'=32,'head'=8] {'ctx'}, dimensions={0}, use_global_device_ids=true | all-gather | bytes 540672 | tf_op jit(solution)/shard_map/all_gather | solution.py:13
  59.4 2.1 fusion.3
  61.4 2.1 fusion.2
  63.5 48.3 %all-gather.3 = f32[32,2,2048]{2,1,0:T(2,128)S(1)} all-gather(f32[1,2,2048]{2,1,0:T(2,128)S(1)} %maximum_bitcast_fusion.1), channel_id=3, replica_groups=mesh['ctx'=32,'head'=8] {'ctx'}, dimensions={0}, use_global_device_ids=true | all-gather | bytes 540672 | tf_op jit(solution)/shard_map/all_gather | solution.py:13
  111.9 1.9 while.12
  113.9 9.2 %multiply_reduce_fusion = (f32[2048]{0:T(1024)S(1)}, f32[2048,1024]{0,1:T(8,128)}, f32[2048,1024]{0,1:T(8,128)}) fusion(f32[2048]{0:T(1024)S(1)} %bitcast.109, f32[2048,1024]{0,1:T(8,128)} %copy-done.1, pred[2048,16]{0,1:T(8,128)(4,1)S(1)} %bitcast.97, bf16[1024,256]{1,0:T(8,128)(2,1)S(1)} %copy-done.7, bf16[2048,256]{1,0:T(8,128)(2,1)S(1)} %copy-done.3), kind=kOutput, calls=%fused_computation.15 | convolution fusion | flops 549451776 | bytes 26001408 | tf_op jit(solution)/shard_map/ld,sd->ls/dot_general | solution.py:57
  123.0 9.1 %multiply_reduce_fusion.1 = (f32[2048]{0:T(1024)S(1)}, f32[2048,1024]{0,1:T(8,128)}, f32[2048,1024]{0,1:T(8,128)}) fusion(f32[2048]{0:T(1024)S(1)} %bitcast.106, f32[2048,1024]{0,1:T(8,128)} %copy-done, pred[2048,16]{0,1:T(8,128)(4,1)S(1)} %bitcast.94, bf16[1024,256]{1,0:T(8,128)(2,1)S(1)} %copy-done.7, bf16[2048,256]{1,0:T(8,128)(2,1)S(1)} %copy-done.3), kind=kOutput, calls=%fused_computation.16 | convolution fusion | flops 549451776 | bytes 26001408 | tf_op jit(solution)/shard_map/ld,sd->ls/dot_general | solution.py:57
  132.2 140.5 %psum.7 = f32[2,2048]{1,0:T(2,128)S(1)} all-reduce(f32[2,2048]{1,0:T(2,128)S(1)} %pad_maximum_fusion.3), channel_id=1, replica_groups=mesh['ctx'=32,'head'=8] {'ctx'}, use_global_device_ids=true, to_apply=%region_9.10 | all-reduce | flops 4096 | bytes 32768 | tf_op jit(solution)/shard_map/psum | solution.py:76
  272.7 8.0 %multiply_convert_fusion = bf16[2048,1024]{0,1:T(8,128)(2,1)S(1)} fusion(f32[2048,1024]{0,1:T(8,128)} %get-tuple-element.57, f32[2048,1024]{0,1:T(8,128)} %get-tuple-element.70, f32[2048]{0:T(1024)S(1)} %bitcast.111), kind=kLoop, calls=%fused_computation.13 | loop fusion | flops 6291456 | bytes 20979712 | tf_op jit(solution)/shard_map/convert_element_type | solution.py:84
  280.7 1.7 convolution_multiply_fusion
  282.4 9.9 %multiply_convert_fusion.1 = bf16[2048,1024]{0,1:T(8,128)(2,1)} fusion(f32[2048,1024]{0,1:T(8,128)} %get-tuple-element.55, f32[2048,1024]{0,1:T(8,128)} %get-tuple-element.71, f32[2048]{0:T(1024)S(1)} %bitcast.108), kind=kLoop, calls=%fused_computation.14 | loop fusion | flops 6291456 | bytes 20979712 | tf_op jit(solution)/shard_map/convert_element_type | solution.py:84
  292.4 3.0 convolution_multiply_fusion.1
  295.6 26.0 %collective-permute-done = f32[2048,256]{0,1:T(8,128)S(1)} collective-permute-done((f32[2048,256]{0,1:T(8,128)S(1)}, f32[2048,256]{0,1:T(8,128)S(1)}, u32[]{:S(2)}, u32[]{:S(2)}) %collective-permute-start) | collective-permute-done | bytes 2097184 | tf_op jit(solution)/shard_map/ppermute | solution.py:105
  322.1 27.5 %collective-permute-done.1 = f32[2048,256]{0,1:T(8,128)S(1)} collective-permute-done((f32[2048,256]{0,1:T(8,128)S(1)}, f32[2048,256]{0,1:T(8,128)S(1)}, u32[]{:S(2)}, u32[]{:S(2)}) %collective-permute-start.1) | collective-permute-done | bytes 2097184 | tf_op jit(solution)/shard_map/ppermute | solution.py:105
  350.1 84.4 %collective-permute-done.2 = f32[2048,256]{0,1:T(8,128)S(1)} collective-permute-done((f32[2048,256]{0,1:T(8,128)S(1)}, f32[2048,256]{0,1:T(8,128)S(1)}, u32[]{:S(2)}, u32[]{:S(2)}) %collective-permute-start.2) | collective-permute-done | bytes 2097184 | tf_op jit(solution)/shard_map/ppermute | solution.py:105
  435.0 48.9 %collective-permute-done.3 = f32[2048,256]{0,1:T(8,128)S(1)} collective-permute-done((f32[2048,256]{0,1:T(8,128)S(1)}, f32[2048,256]{0,1:T(8,128)S(1)}, u32[]{:S(2)}, u32[]{:S(2)}) %collective-permute-start.3) | collective-permute-done | bytes 2097184 | tf_op jit(solution)/shard_map/ppermute | solution.py:105
  485.4 3.4 collective-permute-start.4
  492.2 4.8 all-to-all-start
  497.0 4.6 fusion.13
  501.6 4.6 fusion.10
  507.1 4.8 all-to-all-start.1
  512.8 8.0 %all-to-all-done.1 = bf16[8,128,256]{2,1,0:T(8,128)(2,1)S(1)} async-done(((bf16[8,128,256]{2,1,0:T(8,128)(2,1)}), bf16[8,128,256]{2,1,0:T(8,128)(2,1)S(1)}, u32[]{:S(2)}, u32[]{:S(2)}) %all-to-all-start.1) | async-done | bytes 524320 | tf_op jit(solution)/shard_map/all_to_all | solution.py:110
  521.7 16.4 %collective-permute-done.4 = f32[2048,256]{0,1:T(8,128)} collective-permute-done((f32[2048,256]{0,1:T(8,128)}, f32[2048,256]{0,1:T(8,128)}, u32[]{:S(2)}, u32[]{:S(2)}) %collective-permute-start.4) | collective-permute-done | bytes 2097184 | tf_op jit(solution)/shard_map/ppermute | solution.py:105
  (85 shorter events, 15.9 us)
Async XLA Ops:
  0.6 4.5 copy-start.4
  0.6 4.5 copy-start.5
  5.1 56.3 %copy-start.1 = (f32[2048,1024]{0,1:T(8,128)}, f32[2048,1024]{0,1:T(8,128)S(1)}, u32[]{:S(2)}) copy-start(f32[2048,1024]{0,1:T(8,128)S(1)} %get-tuple-element.67) | copy-start | bytes 25165828
  6.5 57.0 %copy-start = (f32[2048,1024]{0,1:T(8,128)}, f32[2048,1024]{0,1:T(8,128)S(1)}, u32[]{:S(2)}) copy-start(f32[2048,1024]{0,1:T(8,128)S(1)} %get-tuple-element.69) | copy-start | bytes 25165828
  59.3 54.5 %copy-start.3 = (bf16[2048,256]{1,0:T(8,128)(2,1)S(1)}, bf16[2048,256]{1,0:T(8,128)(2,1)}, u32[]{:S(2)}) copy-start(bf16[2048,256]{1,0:T(8,128)(2,1)} %param.11) | copy-start | bytes 3145732
  59.4 54.5 %copy-start.7 = (bf16[1024,256]{1,0:T(8,128)(2,1)S(1)}, bf16[1024,256]{1,0:T(8,128)(2,1)}, u32[]{:S(2)}) copy-start(bf16[1024,256]{1,0:T(8,128)(2,1)} %param.10) | copy-start | bytes 1572868
  295.5 26.1 %collective-permute-start = (f32[2048,256]{0,1:T(8,128)S(1)}, f32[2048,256]{0,1:T(8,128)S(1)}, u32[]{:S(2)}, u32[]{:S(2)}) collective-permute-start(f32[2048,256]{0,1:T(8,128)S(1)} %pad_maximum_fusion), channel_id=1, source_target_pairs={{0,8},{8,0},{16,24},{24,16},{32,40},{40,32},{48,56},{56,48},{64,72... | collective-permute-start | bytes 6291464 | tf_op jit(solution)/shard_map/ppermute | solution.py:105
  322.0 166.8 %copy-start.6 = (bf16[2048,256]{1,0:T(8,128)(2,1)S(1)}, bf16[2048,256]{1,0:T(8,128)(2,1)}, u32[]{:S(2)}) copy-start(bf16[2048,256]{1,0:T(8,128)(2,1)} %param.8) | copy-start | bytes 3145732
  322.0 27.6 %collective-permute-start.1 = (f32[2048,256]{0,1:T(8,128)S(1)}, f32[2048,256]{0,1:T(8,128)S(1)}, u32[]{:S(2)}, u32[]{:S(2)}) collective-permute-start(f32[2048,256]{0,1:T(8,128)S(1)} %fusion.41), channel_id=1, source_target_pairs={{0,16},{8,24},{16,0},{24,8},{32,48},{40,56},{48,32},{56,40},{64,80... | collective-permute-start | bytes 6291464 | tf_op jit(solution)/shard_map/ppermute | solution.py:105
  350.0 140.1 %copy-start.2 = (bf16[2048,1024]{0,1:T(8,128)(2,1)S(1)}, bf16[2048,1024]{0,1:T(8,128)(2,1)}, u32[]{:S(2)}) copy-start(bf16[2048,1024]{0,1:T(8,128)(2,1)} %multiply_convert_fusion.1) | copy-start | bytes 12582916
  350.0 84.5 %collective-permute-start.2 = (f32[2048,256]{0,1:T(8,128)S(1)}, f32[2048,256]{0,1:T(8,128)S(1)}, u32[]{:S(2)}, u32[]{:S(2)}) collective-permute-start(f32[2048,256]{0,1:T(8,128)S(1)} %add.31), channel_id=1, source_target_pairs={{0,32},{8,40},{16,48},{24,56},{32,0},{40,8},{48,16},{56,24},{64,96... | collective-permute-start | bytes 6291464 | tf_op jit(solution)/shard_map/ppermute | solution.py:105
  434.9 49.0 %collective-permute-start.3 = (f32[2048,256]{0,1:T(8,128)S(1)}, f32[2048,256]{0,1:T(8,128)S(1)}, u32[]{:S(2)}, u32[]{:S(2)}) collective-permute-start(f32[2048,256]{0,1:T(8,128)S(1)} %add.32), channel_id=1, source_target_pairs={{0,64},{8,72},{16,80},{24,88},{32,96},{40,104},{48,112},{56,120},{... | collective-permute-start | bytes 6291464 | tf_op jit(solution)/shard_map/ppermute | solution.py:105
  485.4 52.7 %collective-permute-start.4 = (f32[2048,256]{0,1:T(8,128)}, f32[2048,256]{0,1:T(8,128)}, u32[]{:S(2)}, u32[]{:S(2)}) collective-permute-start(f32[2048,256]{0,1:T(8,128)} %add.33), channel_id=1, source_target_pairs={{0,128},{8,136},{16,144},{24,152},{32,160},{40,168},{48,176},{56,1... | collective-permute-start | bytes 6291464 | tf_op jit(solution)/shard_map/ppermute | solution.py:105
  492.2 14.9 %all-to-all-start = ((bf16[8,128,256]{2,1,0:T(8,128)(2,1)}), bf16[8,128,256]{2,1,0:T(8,128)(2,1)S(1)}, u32[]{:S(2)}, u32[]{:S(2)}) async-start(bf16[8,128,256]{2,1,0:T(8,128)(2,1)} %pad_maximum_fusion.1), calls=%async_computation | async-start | bytes 1048576 | tf_op jit(solution)/shard_map/all_to_all | solution.py:109
  507.1 13.7 %all-to-all-start.1 = ((bf16[8,128,256]{2,1,0:T(8,128)(2,1)}), bf16[8,128,256]{2,1,0:T(8,128)(2,1)S(1)}, u32[]{:S(2)}, u32[]{:S(2)}) async-start(bf16[8,128,256]{2,1,0:T(8,128)(2,1)} %pad_maximum_fusion.2), calls=%async_computation.1 | async-start | bytes 1048576 | tf_op jit(solution)/shard_map/all_to_all | solution.py:110
